TPU v7x, 32 devices: a whole 2x2x4 slice. The times are simulated.
32 devices in a mesh: groups: 2 (over y), shard: 16 (over z, x, core).
Axes of the slice: x: 2, y: 2, z: 4, core: 2. Of those that a mesh axis runs over, the one named last changes fastest.
Arguments:
- query_tokens: bfloat16 [1024, 32, 128], P(('groups', 'shard')), parts along dimension 0, may hold values from -0.1875 to 0.1875
- candidates: int32 [1024, 24], P(('groups', 'shard')), parts along dimension 0, may hold values from 0 to 511, as said below
- cand_count: int32 [1024], P(('groups', 'shard')), parts along dimension 0, may hold values from 3 to 24, as said below
- placement_map: int32 [1024], P('groups'), parts along dimension 0, may hold values from 0 to 511, as said below
- passage_base: bfloat16 [1024, 128, 128], P(('groups', 'shard')), parts along dimension 0, may hold values from -6 to 6
- residual_codes: int32 [1024, 128, 128], P(('groups', 'shard')), parts along dimension 0, may hold values from 0 to 3
- passage_lengths: int32 [1024], P(('groups', 'shard')), parts along dimension 0, may hold values from 32 to 128
- bucket_weights: float32 [8], P('groups'), parts along dimension 0, may hold values from -3 to 3
Outputs:
- scores: float32 [1024, 24], P(('groups', 'shard')), parts along dimension 0
There are 2 independent parts, one for each index of `groups`. A program takes and returns all parts, laid end to end along the dimension named above; each array names one. Nothing has to cross between parts.
Inputs may be any that keep to these rules, and one draw needn't show every extreme that they name: In row q the first cand_count[q] entries are distinct passage ids; the devices that store them (device placement_map[id] // 32 of the shard axis) are at most 3, and one device stores at most 8 of them. Of the 32 queries of one device, one storing device (the same for all devices) holds candidates of exactly 9, and every other storing device holds candidates of at most 6. Entries at or beyond cand_count[q] are arbitrary ids. `cand_count`: entries of candidates at or beyond this count are not scored. A permutation: passage id p is row placement_map[p] of the passage store.
All inputs are finite; a program needn't handle non-finite values.
Results may differ from a plain program's by a relative error of at most 0.0003.
Values may be sent and summed in bfloat16 or wider, within the bound.
A program may use at most 64 MiB of HBM per device.

v0:
```python
import jax
import jax.numpy as jnp
from jax import lax
from jax.sharding import PartitionSpec as P

OWNERS_Q = 3
CPQ = 8
epsilon = 1e-06
negative = -1e30


def decode(bases, code_ids, levels):
    residual = jnp.zeros(bases.shape, jnp.float32)
    for bucket in range(4):
        residual = residual + jnp.where(code_ids == bucket, levels[bucket], 0.0)
    summed = bases.astype(jnp.float32) + residual
    inverse_norm = lax.rsqrt(jnp.sum(summed * summed, axis=-1, keepdims=True) + epsilon)
    return (summed * inverse_norm).astype(jnp.bfloat16)


def score_block(query_rows, token_rows, lengths):
    similarity_scores = jnp.einsum(
        "mqd,mkpd->mqkp", query_rows, token_rows, preferred_element_type=jnp.float32
    )
    inside = (
        jnp.arange(token_rows.shape[2], dtype=jnp.int32)[None, None, None, :]
        < lengths[:, None, :, None]
    )
    maxima = jnp.max(jnp.where(inside, similarity_scores, negative), axis=3)
    return jnp.sum(maxima, axis=1)


def score_slots(query_rows, wanted, decoded, lengths):
    item_count = query_rows.shape[0]
    group_size = 16
    padding = -item_count % group_size
    wanted = jnp.maximum(wanted, 0)
    blocks = (item_count + padding) // group_size

    def one_block(bundle):
        query_part, row_part = bundle
        return score_block(query_part, decoded[row_part], lengths[row_part])

    result = lax.map(
        one_block,
        (
            query_rows.reshape(blocks, group_size, query_rows.shape[1], query_rows.shape[2]),
            wanted.reshape(blocks, group_size, wanted.shape[1]),
        ),
    )
    return result.reshape(blocks * group_size, wanted.shape[1])


def pack(present, holder, capacity, query_tokens):
    present_int = present.astype(jnp.int32)
    slot_of = jnp.cumsum(present_int, axis=0) - present_int
    selection_mask = present.T[:, None, :] & (
        slot_of.T[:, None, :] == jnp.arange(capacity, dtype=jnp.int32)[None, :, None]
    )
    outgoing = jnp.einsum(
        "ksq,qtd->kstd",
        selection_mask.astype(jnp.bfloat16),
        query_tokens,
        preferred_element_type=jnp.float32,
    ).astype(jnp.bfloat16)
    target = (
        jnp.sum(
            selection_mask[:, :, :, None].astype(jnp.int32)
            * (jnp.transpose(holder, (1, 0, 2))[:, None, :, :] + 1),
            axis=2,
        )
        - 1
    )
    return (outgoing, target, slot_of)


def local(
    query_tokens,
    candidates,
    cand_count,
    placement_map,
    passage_base,
    residual_codes,
    passage_lengths,
    bucket_weights,
):
    device_count = lax.axis_size("shard")
    query_count, slot_count = candidates.shape
    store_rows = passage_base.shape[0]
    hot_cap = query_count * OWNERS_Q // device_count + 3
    decoded = decode(passage_base, residual_codes, bucket_weights)
    usable = jnp.arange(slot_count, dtype=jnp.int32)[None, :] < cand_count[:, None]
    stored = placement_map[candidates]
    holders = stored // store_rows
    local_row = stored % store_rows
    shared = usable[:, :, None] & usable[:, None, :] & (holders[:, :, None] == holders[:, None, :])
    preceding_total = (
        jnp.arange(slot_count, dtype=jnp.int32)[None, :]
        < jnp.arange(slot_count, dtype=jnp.int32)[:, None]
    )
    within = jnp.sum((shared & preceding_total[None, :, :]).astype(jnp.int32), axis=2)
    owner_ids = jnp.arange(device_count, dtype=jnp.int32)
    matches = usable[:, :, None] & (holders[:, :, None] == owner_ids[None, None, :])
    present = jnp.any(matches, axis=1)
    rank_ids = jnp.arange(CPQ, dtype=jnp.int32)
    holder = (
        jnp.sum(
            jnp.where(
                matches[:, :, :, None]
                & (within[:, :, None, None] == rank_ids[None, None, None, :]),
                local_row[:, :, None, None] + 1,
                0,
            ),
            axis=1,
        )
        - 1
    )
    outgoing, target, slot_of = pack(present, holder, hot_cap, query_tokens)
    queries_in = lax.all_to_all(outgoing, "shard", split_axis=0, concat_axis=0, tiled=True)
    rows_in = lax.all_to_all(
        target.astype(jnp.bfloat16), "shard", split_axis=0, concat_axis=0, tiled=True
    )
    senders = rows_in.shape[0]
    slots_in = rows_in.shape[1]
    flat_queries = queries_in.reshape(senders * slots_in, queries_in.shape[2], queries_in.shape[3])
    row_list_flat = rows_in.astype(jnp.int32).reshape(senders * slots_in, rows_in.shape[2])
    visited = score_slots(flat_queries, row_list_flat, decoded, passage_lengths).reshape(
        senders, slots_in, rows_in.shape[2]
    )
    returned = lax.all_to_all(visited, "shard", split_axis=0, concat_axis=0, tiled=True)
    flattened = returned.reshape(-1)
    pick_slot = jnp.take_along_axis(slot_of, jnp.clip(holders, 0, device_count - 1), axis=1)
    position = holders * (hot_cap * CPQ) + pick_slot * CPQ + within
    result = jnp.take(flattened, position, mode="clip")
    return jnp.where(usable, result, 0.0)


def solution(mesh):
    return jax.shard_map(
        local,
        mesh=mesh,
        in_specs=(
            P(("groups", "shard"), None, None),
            P(("groups", "shard"), None),
            P(("groups", "shard")),
            P("groups"),
            P(("groups", "shard"), None, None),
            P(("groups", "shard"), None, None),
            P(("groups", "shard")),
            P("groups"),
        ),
        out_specs=P(("groups", "shard"), None),
        check_vma=False,
    )
```

profile of v0, /device:TPU:0, one launch (start us, length us, event | category | flops | bytes accessed | tf_op | source)
XLA Modules:
  0.0 154.1 jit_solution(14491903596649840008)
XLA Ops:
  0.0 0.7 iota_compare_fusion.4
  0.8 0.7 compare_select_fusion.2
  1.8 5.0 %gather_fusion.2 = s32[768]{0:T(1024)S(1)} fusion(s32[512]{0:T(512)S(1)} %copy-done, s32[1024]{0:T(1024)S(1)} %pad_clamp_fusion.2), kind=kCustom, calls=%fused_computation.2 | custom fusion | bytes 9216 | tf_op jit(solution)/shard_map/gather | solution.py:93
  7.0 0.2 convert_reduce_fusion
  7.5 0.3 select_reduce_fusion.1
  7.8 2.5 %multiply_reduce_fusion.1 = s32[16,9,8]{2,1,0:T(8,128)S(1)} fusion(s32[16,32,8]{1,2,0:T(8,128)S(1)} %bitcast.58, s32[16,9,32]{2,1,0:T(8,128)S(1)} %copy.110), kind=kLoop, calls=%fused_computation.18 | loop fusion | flops 72576 | bytes 39424 | tf_op jit(solution)/shard_map/reduce_sum | solution.py:67
  10.3 0.1 copy.113
  10.5 0.7 copy.114
  11.2 7.4 %all-to-all-start = ((bf16[16,9,8]{1,2,0:T(8,128)(2,1)}), bf16[16,9,8]{1,2,0:T(8,128)(2,1)S(1)}, u32[]{:S(2)}, u32[]{:S(2)}) async-start(bf16[16,9,8]{1,2,0:T(8,128)(2,1)} %copy.114), calls=%async_computation | async-start | bytes 65536 | tf_op jit(solution)/shard_map/all_to_all | solution.py:120
  18.6 0.5 convolution_convert_fusion
  19.1 1.3 copy.118
  20.4 4.9 %all-to-all-done = bf16[16,9,8]{1,2,0:T(8,128)(2,1)S(1)} async-done(((bf16[16,9,8]{1,2,0:T(8,128)(2,1)}), bf16[16,9,8]{1,2,0:T(8,128)(2,1)S(1)}, u32[]{:S(2)}, u32[]{:S(2)}) %all-to-all-start) | async-done | bytes 2336 | tf_op jit(solution)/shard_map/all_to_all | solution.py:120
  25.2 4.4 %all-to-all-start.1 = ((bf16[16,9,32,128]{3,2,1,0:T(8,128)(2,1)}), bf16[16,9,32,128]{3,2,1,0:T(8,128)(2,1)}, u32[]{:S(2)}, u32[]{:S(2)}) async-start(bf16[16,9,32,128]{3,2,1,0:T(8,128)(2,1)} %copy.118), calls=%async_computation.1 | async-start | bytes 2359296 | tf_op jit(solution)/shard_map/all_to_all | solution.py:119
  30.0 5.1 %gather_fusion.4 = s32[768]{0:T(1024)S(1)} fusion(s32[32,16]{1,0:T(8,128)S(1)} %convert_subtract_fusion, s32[768]{0:T(1024)S(1)} %reshape.292), kind=kCustom, calls=%fused_computation.4 | custom fusion | bytes 12288 | tf_op jit(solution)/shard_map/jit(take_along_axis)/gather | solution.py:132
  35.5 0.6 fusion.18
  36.2 4.8 %multiply_reduce_fusion = f32[32,128]{1,0:T(8,128)S(1)} fusion(f32[]{:T(128)} %bitcast.17, s32[32,128,128]{2,1,0:T(8,128)S(1)} %copy-done.2, f32[]{:T(128)} %bitcast.16, f32[]{:T(128)} %bitcast.15, f32[]{:T(128)} %bitcast.14, bf16[32,128,128]{2,1,0:T(8,128)(2,1)} %param.14), kind=kLoop, calls=%fused_computation.14 | loop fusion | flops 7860224 | bytes 3162128 | tf_op jit(solution)/shard_map/reduce_sum | solution.py:17
  41.0 4.6 %multiply_convert_fusion = bf16[32,128,128]{2,1,0:T(8,128)(2,1)S(1)} fusion(f32[32,128]{1,0:T(8,128)S(1)} %add_rsqrt_fusion, f32[]{:T(128)} %bitcast.17, s32[32,128,128]{2,1,0:T(8,128)S(1)} %copy-done.2, f32[]{:T(128)} %bitcast.16, f32[]{:T(128)} %bitcast.15, f32[]{:T(128)} %bitcast.14, bf16[32,128,128]{2,1,0:T(8,128)(2,1)} %param.14), kind=kLoop, calls=%fused_computation.13 | loop fusion | flops 7864320 | bytes 4210704 | tf_op jit(solution)/shard_map/convert_element_type | solution.py:18
  45.6 0.1 copy.115
  45.8 0.1 copy.116
  45.9 0.1 max.16
  46.0 8.7 %all-to-all-done.1 = bf16[16,9,32,128]{3,2,1,0:T(8,128)(2,1)} async-done(((bf16[16,9,32,128]{3,2,1,0:T(8,128)(2,1)}), bf16[16,9,32,128]{3,2,1,0:T(8,128)(2,1)}, u32[]{:S(2)}, u32[]{:S(2)}) %all-to-all-start.1) | async-done | bytes 1179680 | tf_op jit(solution)/shard_map/all_to_all | solution.py:119
  54.7 78.7 %while.10 = (s32[]{:T(128)}, f32[9,16,8]{1,0,2:T(8,128)S(1)}, s32[9,16,8]{1,0,2:T(8,128)S(1)}, s32[32]{0:T(128)S(1)}, bf16[9,16,32,128]{3,2,1,0:T(8,128)(2,1)}, ...) while((s32[]{:T(128)}, f32[9,16,8]{1,0,2:T(8,128)S(1)}, ...), condition=%wide.region_9.10_spmd, body=%wide.region_6.9_spmd.sunk | while | flops 135283968 | bytes 12794485 | solution.py:44
  54.9 1.2 gather_fusion.1
  56.2 0.1 iota_compare_fusion.7
  56.3 3.0 %gather_fusion = bf16[128,128,128]{2,1,0:T(8,128)(2,1)} fusion(bf16[32,128,128]{2,1,0:T(8,128)(2,1)S(1)} %get-tuple-element.148, s32[1024]{0:T(1024)S(1)} %pad_clamp_fusion.4), kind=kCustom, calls=%fused_computation.1.clone.1 | custom fusion | bytes 8389120 | tf_op jit(solution)/shard_map/while/body/eval_jaxpr/gather | solution.py:42
  59.3 3.9 %select_reduce_fusion.3 = f32[16,32,8]{1,2,0:T(8,128)S(1)} fusion(bf16[16,8,128,128]{3,2,1,0:T(8,128)(2,1)} %bitcast.55, pred[16,8,128]{2,1,0:T(8,128)(4,1)S(1)} %iota_compare_fusion.7, bf16[9,16,32,128]{3,2,1,0:T(8,128)(2,1)} %get-tuple-element.147, s32[]{:T(128)S(6)} %copy.149), kind=kOutput, calls=%fused_computation.5.clone.1 | convolution fusion | flops 135262208 | bytes 4358148 | tf_op jit(solution)/shard_map/while/body/eval_jaxpr/mqd,mkpd->mqkp/dot_general | solution.py:22
  63.6 1.2 gather_fusion.1
  64.9 0.1 iota_compare_fusion.7
  65.0 3.0 %gather_fusion = bf16[128,128,128]{2,1,0:T(8,128)(2,1)} fusion(bf16[32,128,128]{2,1,0:T(8,128)(2,1)S(1)} %get-tuple-element.148, s32[1024]{0:T(1024)S(1)} %pad_clamp_fusion.4), kind=kCustom, calls=%fused_computation.1.clone.1 | custom fusion | bytes 8389120 | tf_op jit(solution)/shard_map/while/body/eval_jaxpr/gather | solution.py:42
  68.1 3.9 %select_reduce_fusion.3 = f32[16,32,8]{1,2,0:T(8,128)S(1)} fusion(bf16[16,8,128,128]{3,2,1,0:T(8,128)(2,1)} %bitcast.55, pred[16,8,128]{2,1,0:T(8,128)(4,1)S(1)} %iota_compare_fusion.7, bf16[9,16,32,128]{3,2,1,0:T(8,128)(2,1)} %get-tuple-element.147, s32[]{:T(128)S(6)} %copy.149), kind=kOutput, calls=%fused_computation.5.clone.1 | convolution fusion | flops 135262208 | bytes 4358148 | tf_op jit(solution)/shard_map/while/body/eval_jaxpr/mqd,mkpd->mqkp/dot_general | solution.py:22
  72.4 1.2 gather_fusion.1
  73.7 0.1 iota_compare_fusion.7
  73.8 3.0 %gather_fusion = bf16[128,128,128]{2,1,0:T(8,128)(2,1)} fusion(bf16[32,128,128]{2,1,0:T(8,128)(2,1)S(1)} %get-tuple-element.148, s32[1024]{0:T(1024)S(1)} %pad_clamp_fusion.4), kind=kCustom, calls=%fused_computation.1.clone.1 | custom fusion | bytes 8389120 | tf_op jit(solution)/shard_map/while/body/eval_jaxpr/gather | solution.py:42
  76.8 3.9 %select_reduce_fusion.3 = f32[16,32,8]{1,2,0:T(8,128)S(1)} fusion(bf16[16,8,128,128]{3,2,1,0:T(8,128)(2,1)} %bitcast.55, pred[16,8,128]{2,1,0:T(8,128)(4,1)S(1)} %iota_compare_fusion.7, bf16[9,16,32,128]{3,2,1,0:T(8,128)(2,1)} %get-tuple-element.147, s32[]{:T(128)S(6)} %copy.149), kind=kOutput, calls=%fused_computation.5.clone.1 | convolution fusion | flops 135262208 | bytes 4358148 | tf_op jit(solution)/shard_map/while/body/eval_jaxpr/mqd,mkpd->mqkp/dot_general | solution.py:22
  81.1 1.2 gather_fusion.1
  82.4 0.1 iota_compare_fusion.7
  82.5 3.0 %gather_fusion = bf16[128,128,128]{2,1,0:T(8,128)(2,1)} fusion(bf16[32,128,128]{2,1,0:T(8,128)(2,1)S(1)} %get-tuple-element.148, s32[1024]{0:T(1024)S(1)} %pad_clamp_fusion.4), kind=kCustom, calls=%fused_computation.1.clone.1 | custom fusion | bytes 8389120 | tf_op jit(solution)/shard_map/while/body/eval_jaxpr/gather | solution.py:42
  85.6 3.9 %select_reduce_fusion.3 = f32[16,32,8]{1,2,0:T(8,128)S(1)} fusion(bf16[16,8,128,128]{3,2,1,0:T(8,128)(2,1)} %bitcast.55, pred[16,8,128]{2,1,0:T(8,128)(4,1)S(1)} %iota_compare_fusion.7, bf16[9,16,32,128]{3,2,1,0:T(8,128)(2,1)} %get-tuple-element.147, s32[]{:T(128)S(6)} %copy.149), kind=kOutput, calls=%fused_computation.5.clone.1 | convolution fusion | flops 135262208 | bytes 4358148 | tf_op jit(solution)/shard_map/while/body/eval_jaxpr/mqd,mkpd->mqkp/dot_general | solution.py:22
  89.9 1.2 gather_fusion.1
  91.3 3.0 %gather_fusion = bf16[128,128,128]{2,1,0:T(8,128)(2,1)} fusion(bf16[32,128,128]{2,1,0:T(8,128)(2,1)S(1)} %get-tuple-element.148, s32[1024]{0:T(1024)S(1)} %pad_clamp_fusion.4), kind=kCustom, calls=%fused_computation.1.clone.1 | custom fusion | bytes 8389120 | tf_op jit(solution)/shard_map/while/body/eval_jaxpr/gather | solution.py:42
  94.3 3.9 %select_reduce_fusion.3 = f32[16,32,8]{1,2,0:T(8,128)S(1)} fusion(bf16[16,8,128,128]{3,2,1,0:T(8,128)(2,1)} %bitcast.55, pred[16,8,128]{2,1,0:T(8,128)(4,1)S(1)} %iota_compare_fusion.7, bf16[9,16,32,128]{3,2,1,0:T(8,128)(2,1)} %get-tuple-element.147, s32[]{:T(128)S(6)} %copy.149), kind=kOutput, calls=%fused_computation.5.clone.1 | convolution fusion | flops 135262208 | bytes 4358148 | tf_op jit(solution)/shard_map/while/body/eval_jaxpr/mqd,mkpd->mqkp/dot_general | solution.py:22
  98.6 1.2 gather_fusion.1
  99.9 0.1 iota_compare_fusion.7
  100.0 3.0 %gather_fusion = bf16[128,128,128]{2,1,0:T(8,128)(2,1)} fusion(bf16[32,128,128]{2,1,0:T(8,128)(2,1)S(1)} %get-tuple-element.148, s32[1024]{0:T(1024)S(1)} %pad_clamp_fusion.4), kind=kCustom, calls=%fused_computation.1.clone.1 | custom fusion | bytes 8389120 | tf_op jit(solution)/shard_map/while/body/eval_jaxpr/gather | solution.py:42
  103.1 3.9 %select_reduce_fusion.3 = f32[16,32,8]{1,2,0:T(8,128)S(1)} fusion(bf16[16,8,128,128]{3,2,1,0:T(8,128)(2,1)} %bitcast.55, pred[16,8,128]{2,1,0:T(8,128)(4,1)S(1)} %iota_compare_fusion.7, bf16[9,16,32,128]{3,2,1,0:T(8,128)(2,1)} %get-tuple-element.147, s32[]{:T(128)S(6)} %copy.149), kind=kOutput, calls=%fused_computation.5.clone.1 | convolution fusion | flops 135262208 | bytes 4358148 | tf_op jit(solution)/shard_map/while/body/eval_jaxpr/mqd,mkpd->mqkp/dot_general | solution.py:22
  107.4 1.2 gather_fusion.1
  108.7 0.1 iota_compare_fusion.7
  108.8 3.0 %gather_fusion = bf16[128,128,128]{2,1,0:T(8,128)(2,1)} fusion(bf16[32,128,128]{2,1,0:T(8,128)(2,1)S(1)} %get-tuple-element.148, s32[1024]{0:T(1024)S(1)} %pad_clamp_fusion.4), kind=kCustom, calls=%fused_computation.1.clone.1 | custom fusion | bytes 8389120 | tf_op jit(solution)/shard_map/while/body/eval_jaxpr/gather | solution.py:42
  111.8 3.9 %select_reduce_fusion.3 = f32[16,32,8]{1,2,0:T(8,128)S(1)} fusion(bf16[16,8,128,128]{3,2,1,0:T(8,128)(2,1)} %bitcast.55, pred[16,8,128]{2,1,0:T(8,128)(4,1)S(1)} %iota_compare_fusion.7, bf16[9,16,32,128]{3,2,1,0:T(8,128)(2,1)} %get-tuple-element.147, s32[]{:T(128)S(6)} %copy.149), kind=kOutput, calls=%fused_computation.5.clone.1 | convolution fusion | flops 135262208 | bytes 4358148 | tf_op jit(solution)/shard_map/while/body/eval_jaxpr/mqd,mkpd->mqkp/dot_general | solution.py:22
  116.1 1.2 gather_fusion.1
  117.4 0.1 iota_compare_fusion.7
  117.5 3.0 %gather_fusion = bf16[128,128,128]{2,1,0:T(8,128)(2,1)} fusion(bf16[32,128,128]{2,1,0:T(8,128)(2,1)S(1)} %get-tuple-element.148, s32[1024]{0:T(1024)S(1)} %pad_clamp_fusion.4), kind=kCustom, calls=%fused_computation.1.clone.1 | custom fusion | bytes 8389120 | tf_op jit(solution)/shard_map/while/body/eval_jaxpr/gather | solution.py:42
  120.6 3.9 %select_reduce_fusion.3 = f32[16,32,8]{1,2,0:T(8,128)S(1)} fusion(bf16[16,8,128,128]{3,2,1,0:T(8,128)(2,1)} %bitcast.55, pred[16,8,128]{2,1,0:T(8,128)(4,1)S(1)} %iota_compare_fusion.7, bf16[9,16,32,128]{3,2,1,0:T(8,128)(2,1)} %get-tuple-element.147, s32[]{:T(128)S(6)} %copy.149), kind=kOutput, calls=%fused_computation.5.clone.1 | convolution fusion | flops 135262208 | bytes 4358148 | tf_op jit(solution)/shard_map/while/body/eval_jaxpr/mqd,mkpd->mqkp/dot_general | solution.py:22
  124.9 1.2 gather_fusion.1
  126.2 0.1 iota_compare_fusion.7
  126.3 3.0 %gather_fusion = bf16[128,128,128]{2,1,0:T(8,128)(2,1)} fusion(bf16[32,128,128]{2,1,0:T(8,128)(2,1)S(1)} %get-tuple-element.148, s32[1024]{0:T(1024)S(1)} %pad_clamp_fusion.4), kind=kCustom, calls=%fused_computation.1.clone.1 | custom fusion | bytes 8389120 | tf_op jit(solution)/shard_map/while/body/eval_jaxpr/gather | solution.py:42
  129.3 3.9 %select_reduce_fusion.3 = f32[16,32,8]{1,2,0:T(8,128)S(1)} fusion(bf16[16,8,128,128]{3,2,1,0:T(8,128)(2,1)} %bitcast.55, pred[16,8,128]{2,1,0:T(8,128)(4,1)S(1)} %iota_compare_fusion.7, bf16[9,16,32,128]{3,2,1,0:T(8,128)(2,1)} %get-tuple-element.147, s32[]{:T(128)S(6)} %copy.149), kind=kOutput, calls=%fused_computation.5.clone.1 | convolution fusion | flops 135262208 | bytes 4358148 | tf_op jit(solution)/shard_map/while/body/eval_jaxpr/mqd,mkpd->mqkp/dot_general | solution.py:22
  133.5 0.6 copy.121
  134.2 7.4 %all-to-all-start.2 = ((f32[16,9,8]{1,2,0:T(8,128)}), f32[16,9,8]{1,2,0:T(8,128)S(1)}, u32[]{:S(2)}, u32[]{:S(2)}) async-start(f32[16,9,8]{1,2,0:T(8,128)} %copy.121), calls=%async_computation.2 | async-start | bytes 131072 | tf_op jit(solution)/shard_map/all_to_all | solution.py:130
  141.6 6.9 %all-to-all-done.2 = f32[16,9,8]{1,2,0:T(8,128)S(1)} async-done(((f32[16,9,8]{1,2,0:T(8,128)}), f32[16,9,8]{1,2,0:T(8,128)S(1)}, u32[]{:S(2)}, u32[]{:S(2)}) %all-to-all-start.2) | async-done | bytes 4640 | tf_op jit(solution)/shard_map/all_to_all | solution.py:130
  148.5 0.2 copy.122
  148.6 0.1 reshape.259
  148.7 4.5 %gather_fusion.3 = f32[768]{0:T(1024)S(1)} fusion(f32[1152]{0:T(1024)S(1)} %reshape.259, s32[1024]{0:T(1024)S(1)} %pad_clamp_fusion.1), kind=kCustom, calls=%fused_computation.3 | custom fusion | bytes 9216 | tf_op jit(solution)/shard_map/jit(_take)/gather | solution.py:134
  153.4 0.7 copy.130
  (130 shorter events, 5.9 us)
Async XLA Ops:
  0.0 1.7 %copy-start = (s32[512]{0:T(512)S(1)}, s32[512]{0:T(512)}, u32[]{:S(2)}) copy-start(s32[512]{0:T(512)} %param.13) | copy-start | bytes 6148
  1.7 16.9 %copy-start.3 = (bf16[32,32,128]{2,1,0:T(8,128)(2,1)S(1)}, bf16[32,32,128]{2,1,0:T(8,128)(2,1)}, u32[]{:S(2)}) copy-start(bf16[32,32,128]{2,1,0:T(8,128)(2,1)} %param.10) | copy-start | bytes 786436
  11.2 14.0 %all-to-all-start = ((bf16[16,9,8]{1,2,0:T(8,128)(2,1)}), bf16[16,9,8]{1,2,0:T(8,128)(2,1)S(1)}, u32[]{:S(2)}, u32[]{:S(2)}) async-start(bf16[16,9,8]{1,2,0:T(8,128)(2,1)} %copy.114), calls=%async_computation | async-start | bytes 65536 | tf_op jit(solution)/shard_map/all_to_all | solution.py:120
  25.2 29.5 %all-to-all-start.1 = ((bf16[16,9,32,128]{3,2,1,0:T(8,128)(2,1)}), bf16[16,9,32,128]{3,2,1,0:T(8,128)(2,1)}, u32[]{:S(2)}, u32[]{:S(2)}) async-start(bf16[16,9,32,128]{3,2,1,0:T(8,128)(2,1)} %copy.118), calls=%async_computation.1 | async-start | bytes 2359296 | tf_op jit(solution)/shard_map/all_to_all | solution.py:119
  30.0 5.5 %copy-start.4 = (f32[4]{0:T(128)S(1)}, f32[4]{0:T(128)}, u32[]{:S(2)}) copy-start(f32[4]{0:T(128)} %param.17) | copy-start | bytes 52
  30.0 6.2 %copy-start.2 = (s32[32,128,128]{2,1,0:T(8,128)S(1)}, s32[32,128,128]{2,1,0:T(8,128)}, u32[]{:S(2)}) copy-start(s32[32,128,128]{2,1,0:T(8,128)} %param.15) | copy-start | bytes 6291460
  41.0 13.7 %copy-start.1 = (s32[32]{0:T(128)S(1)}, s32[32]{0:T(128)}, u32[]{:S(2)}) copy-start(s32[32]{0:T(128)} %param.16) | copy-start | bytes 388
  134.2 14.3 %all-to-all-start.2 = ((f32[16,9,8]{1,2,0:T(8,128)}), f32[16,9,8]{1,2,0:T(8,128)S(1)}, u32[]{:S(2)}, u32[]{:S(2)}) async-start(f32[16,9,8]{1,2,0:T(8,128)} %copy.121), calls=%async_computation.2 | async-start | bytes 131072 | tf_op jit(solution)/shard_map/all_to_all | solution.py:130
  148.7 4.6 %copy-start.5 = (s32[32]{0:T(128)S(1)}, s32[32]{0:T(128)}, u32[]{:S(2)}) copy-start(s32[32]{0:T(128)} %param.12) | copy-start | bytes 388
where the time goes:
time: 155 us; the launch traced here: 154 us
  local copies, waits for them, and re-layouts  62 us (40%)
  matrix products  35.5 us (23%)
  waiting for transfers between devices  20.4 us (13%)
  starting transfers between devices  19.2 us (12%)
  other arithmetic  16 us (10%)
    gather x27, local copies, waits for them, and re-layouts, one_block(): return score_block(query_part, decoded[row_part], lengths[row_part])  38.8 us
    dot_general x9, matrix products, score_block(): jnp.einsum('mqd,mkpd->mqkp', query_rows, token_rows, preferred_element_ty...  35 us
    all_to_all x1, waiting for transfers between devices, local(): lax.all_to_all(outgoing, 'shard', split_axis=0, concat_axis=0, tiled=True)  8.68 us
    all_to_all x1, starting transfers between devices, local(): lax.all_to_all(visited, 'shard', split_axis=0, concat_axis=0, tiled=True)  7.39 us
    all_to_all x1, starting transfers between devices, local(): lax.all_to_all(target.astype(jnp.bfloat16), 'shard', split_axis=0, concat...  7.39 us
    all_to_all x1, waiting for transfers between devices, local(): lax.all_to_all(visited, 'shard', split_axis=0, concat_axis=0, tiled=True)  6.88 us
    gather x5, local copies, waits for them, and re-layouts, local(): jnp.take_along_axis(slot_of, jnp.clip(holders, 0, device_count - 1), axis=1)  5.46 us
    gather x5, local copies, waits for them, and re-layouts, local(): stored = placement_map[candidates]  5.3 us
  transfers between devices with their start and end apart: 3, of which 3 were waited for; matrix products, arithmetic and copies ran while one was open for 12% of the time, Pallas kernels for 0%

commit v1 on v0

--- a/solution.py
+++ b/solution.py
@@ -7,6 +7,18 @@
 CPQ = 8
 epsilon = 1e-06
 negative = -1e30
+
+
+def rotated_exchange(value, axis, split, join):
+    ways, here = (lax.axis_size(axis), lax.axis_index(axis))
+    width = value.shape[split] // ways
+    turned = jnp.roll(value, -here * width, axis=split)
+    got = [lax.slice_in_dim(turned, 0, width, axis=split)]
+    for far in range(1, ways):
+        sent = lax.slice_in_dim(turned, far * width, (far + 1) * width, axis=split)
+        got.append(lax.ppermute(sent, axis, [(d, (d + far) % ways) for d in range(ways)]))
+    line = jnp.concatenate(got[::-1], axis=join)
+    return jnp.roll(line, (here + 1) * got[0].shape[join], axis=join)
 
 
 def decode(bases, code_ids, levels):
@@ -117,9 +129,7 @@
     )
     outgoing, target, slot_of = pack(present, holder, hot_cap, query_tokens)
     queries_in = lax.all_to_all(outgoing, "shard", split_axis=0, concat_axis=0, tiled=True)
-    rows_in = lax.all_to_all(
-        target.astype(jnp.bfloat16), "shard", split_axis=0, concat_axis=0, tiled=True
-    )
+    rows_in = rotated_exchange(target.astype(jnp.bfloat16), "shard", 0, 0)
     senders = rows_in.shape[0]
     slots_in = rows_in.shape[1]
     flat_queries = queries_in.reshape(senders * slots_in, queries_in.shape[2], queries_in.shape[3])

time: 155 us -> 160 us (1.032)
  starting transfers between devices: 19.2 us -> 36.1 us
  waiting for transfers between devices: 20.4 us -> 8.37 us
    ppermute x0 -> x15, starting transfers between devices: none -> 22.8 us  [rotated_exchange(): lax.ppermute(sent, axis, [(d, (d + far) % ways) for d in range(ways)])]
    all_to_all x1, waiting for transfers between devices: 8.68 us -> 0.01 us  [local(): lax.all_to_all(outgoing, 'shard', split_axis=0, concat_axis=0, tiled=True)]
    all_to_all x1 -> x0, starting transfers between devices: 7.39 us -> none  [local(): lax.all_to_all(target.astype(jnp.bfloat16), 'shard', split_axis=0, concat...]
    all_to_all x1 -> x0, waiting for transfers between devices: 4.85 us -> none  [local(): lax.all_to_all(target.astype(jnp.bfloat16), 'shard', split_axis=0, concat...]
    all_to_all x1, starting transfers between devices: 4.39 us -> 7.43 us  [local(): lax.all_to_all(outgoing, 'shard', split_axis=0, concat_axis=0, tiled=True)]
  transfers between devices with their start and end apart: 3 -> 17, of which waited for: 3 -> 3; matrix products, arithmetic and copies ran while one was open for 12% -> 13% of each run, Pallas kernels for 0% -> 0%
where the time goes in v1:
time: 160 us; the launch traced here: 159 us
  local copies, waits for them, and re-layouts  62.3 us (39%)
  starting transfers between devices  36.1 us (23%)
  matrix products  35.5 us (22%)
  other arithmetic  16.1 us (10%)
  waiting for transfers between devices  8.37 us (5%)
    gather x27, local copies, waits for them, and re-layouts, one_block(): return score_block(query_part, decoded[row_part], lengths[row_part])  39 us
    dot_general x9, matrix products, score_block(): jnp.einsum('mqd,mkpd->mqkp', query_rows, token_rows, preferred_element_ty...  35 us
    ppermute x15, starting transfers between devices, rotated_exchange(): lax.ppermute(sent, axis, [(d, (d + far) % ways) for d in range(ways)])  22.8 us
    all_to_all x1, starting transfers between devices, local(): lax.all_to_all(outgoing, 'shard', split_axis=0, concat_axis=0, tiled=True)  7.43 us
    all_to_all x1, waiting for transfers between devices, local(): lax.all_to_all(visited, 'shard', split_axis=0, concat_axis=0, tiled=True)  6.88 us
    all_to_all x1, starting transfers between devices, local(): lax.all_to_all(visited, 'shard', split_axis=0, concat_axis=0, tiled=True)  5.8 us
    gather x5, local copies, waits for them, and re-layouts, local(): jnp.take_along_axis(slot_of, jnp.clip(holders, 0, device_count - 1), axis=1)  5.46 us
    gather x5, local copies, waits for them, and re-layouts, local(): stored = placement_map[candidates]  5.3 us
  transfers between devices with their start and end apart: 17, of which 3 were waited for; matrix products, arithmetic and copies ran while one was open for 13% of the time, Pallas kernels for 0%

profile of v1, /device:TPU:0, one launch (start us, length us, event | category | flops | bytes accessed | tf_op | source)
XLA Modules:
  0.0 159.4 jit_solution(14190725806485052736)
XLA Ops:
  0.0 0.7 iota_compare_fusion.4
  0.8 0.7 compare_select_fusion.2
  1.8 5.0 %gather_fusion.2 = s32[768]{0:T(1024)S(1)} fusion(s32[512]{0:T(512)S(1)} %copy-done, s32[1024]{0:T(1024)S(1)} %pad_clamp_fusion.2), kind=kCustom, calls=%fused_computation.2 | custom fusion | bytes 9216 | tf_op jit(solution)/shard_map/gather | solution.py:105
  7.2 0.5 convolution_convert_fusion
  7.7 1.3 copy.117
  9.0 7.4 %all-to-all-start = ((bf16[16,9,32,128]{3,2,1,0:T(8,128)(2,1)}), bf16[16,9,32,128]{3,2,1,0:T(8,128)(2,1)}, u32[]{:S(2)}, u32[]{:S(2)}) async-start(bf16[16,9,32,128]{3,2,1,0:T(8,128)(2,1)} %copy.117), calls=%async_computation | async-start | bytes 2359296 | tf_op jit(solution)/shard_map/all_to_all | solution.py:131
  16.5 0.2 convert_reduce_fusion
  16.8 0.3 select_reduce_fusion.1
  17.1 2.5 %multiply_reduce_fusion.1 = s32[16,9,8]{2,1,0:T(8,128)S(1)} fusion(s32[16,32,8]{1,2,0:T(8,128)S(1)} %bitcast.58, s32[16,9,32]{2,1,0:T(8,128)S(1)} %copy.111), kind=kLoop, calls=%fused_computation.18 | loop fusion | flops 72576 | bytes 39424 | tf_op jit(solution)/shard_map/reduce_sum | solution.py:79
  19.8 0.8 fusion.18
  20.7 0.3 collective-permute-start.14
  21.0 1.6 %collective-permute-start.13 = (bf16[1,9,8]{0,2,1:T(8,128)(2,1)}, bf16[1,9,8]{0,2,1:T(8,128)(2,1)S(1)}, u32[]{:S(2)}, u32[]{:S(2)}) collective-permute-start(bf16[1,9,8]{0,2,1:T(8,128)(2,1)} %get-tuple-element.83), channel_id=1, source_target_pairs={{0,2},{1,3},{2,4},{3,5},{4,6},{5,7},{6,8},{7,9},{8,10},{9,11},{10,... | collective-permute-start | bytes 440 | tf_op jit(solution)/shard_map/ppermute | solution.py:19
  22.6 2.3 %collective-permute-start.12 = (bf16[1,9,8]{0,2,1:T(8,128)(2,1)}, bf16[1,9,8]{0,2,1:T(8,128)(2,1)S(1)}, u32[]{:S(2)}, u32[]{:S(2)}) collective-permute-start(bf16[1,9,8]{0,2,1:T(8,128)(2,1)} %get-tuple-element.84), channel_id=1, source_target_pairs={{0,3},{1,4},{2,5},{3,6},{4,7},{5,8},{6,9},{7,10},{8,11},{9,12},{10... | collective-permute-start | bytes 440 | tf_op jit(solution)/shard_map/ppermute | solution.py:19
  24.9 1.5 collective-permute-start.11
  26.9 5.1 %gather_fusion.4 = s32[768]{0:T(1024)S(1)} fusion(s32[32,16]{1,0:T(8,128)S(1)} %convert_subtract_fusion, s32[768]{0:T(1024)S(1)} %reshape.292), kind=kCustom, calls=%fused_computation.4 | custom fusion | bytes 12288 | tf_op jit(solution)/shard_map/jit(take_along_axis)/gather | solution.py:142
  32.3 0.7 fusion.19
  33.0 4.8 %multiply_reduce_fusion = f32[32,128]{1,0:T(8,128)S(1)} fusion(f32[]{:T(128)} %bitcast.17, s32[32,128,128]{2,1,0:T(8,128)S(1)} %copy-done.2, f32[]{:T(128)} %bitcast.16, f32[]{:T(128)} %bitcast.15, f32[]{:T(128)} %bitcast.14, bf16[32,128,128]{2,1,0:T(8,128)(2,1)} %param.16), kind=kLoop, calls=%fused_computation.14 | loop fusion | flops 7860224 | bytes 3162128 | tf_op jit(solution)/shard_map/reduce_sum | solution.py:29
  37.7 4.6 %multiply_convert_fusion = bf16[32,128,128]{2,1,0:T(8,128)(2,1)S(1)} fusion(f32[32,128]{1,0:T(8,128)S(1)} %add_rsqrt_fusion, f32[]{:T(128)} %bitcast.17, s32[32,128,128]{2,1,0:T(8,128)S(1)} %copy-done.2, f32[]{:T(128)} %bitcast.16, f32[]{:T(128)} %bitcast.15, f32[]{:T(128)} %bitcast.14, bf16[32,128,128]{2,1,0:T(8,128)(2,1)} %param.16), kind=kLoop, calls=%fused_computation.13 | loop fusion | flops 7864320 | bytes 4210704 | tf_op jit(solution)/shard_map/convert_element_type | solution.py:30
  42.4 1.5 collective-permute-start.9
  43.9 4.1 %collective-permute-start.8 = (bf16[1,9,8]{0,2,1:T(8,128)(2,1)S(1)}, bf16[1,9,8]{0,2,1:T(8,128)(2,1)S(1)}, u32[]{:S(2)}, u32[]{:S(2)}) collective-permute-start(bf16[1,9,8]{0,2,1:T(8,128)(2,1)S(1)} %get-tuple-element.88), channel_id=1, source_target_pairs={{0,7},{1,8},{2,9},{3,10},{4,11},{5,12},{6,13},{7,14},{8,15},{9,0},... | collective-permute-start | bytes 440 | tf_op jit(solution)/shard_map/ppermute | solution.py:19
  48.0 0.6 collective-permute-start.7
  48.5 2.2 %collective-permute-start.6 = (bf16[1,9,8]{0,2,1:T(8,128)(2,1)S(1)}, bf16[1,9,8]{0,2,1:T(8,128)(2,1)S(1)}, u32[]{:S(2)}, u32[]{:S(2)}) collective-permute-start(bf16[1,9,8]{0,2,1:T(8,128)(2,1)S(1)} %get-tuple-element.90), channel_id=1, source_target_pairs={{0,9},{1,10},{2,11},{3,12},{4,13},{5,14},{6,15},{7,0},{8,1},{9,2},... | collective-permute-start | bytes 440 | tf_op jit(solution)/shard_map/ppermute | solution.py:19
  50.8 2.7 %collective-permute-start.5 = (bf16[1,9,8]{0,2,1:T(8,128)(2,1)S(1)}, bf16[1,9,8]{0,2,1:T(8,128)(2,1)S(1)}, u32[]{:S(2)}, u32[]{:S(2)}) collective-permute-start(bf16[1,9,8]{0,2,1:T(8,128)(2,1)S(1)} %get-tuple-element.91), channel_id=1, source_target_pairs={{0,10},{1,11},{2,12},{3,13},{4,14},{5,15},{6,0},{7,1},{8,2},{9,3},... | collective-permute-start | bytes 440 | tf_op jit(solution)/shard_map/ppermute | solution.py:19
  53.4 0.7 collective-permute-start.4
  54.2 1.8 %collective-permute-start.3 = (bf16[1,9,8]{0,2,1:T(8,128)(2,1)S(1)}, bf16[1,9,8]{0,2,1:T(8,128)(2,1)S(1)}, u32[]{:S(2)}, u32[]{:S(2)}) collective-permute-start(bf16[1,9,8]{0,2,1:T(8,128)(2,1)S(1)} %get-tuple-element.93), channel_id=1, source_target_pairs={{0,12},{1,13},{2,14},{3,15},{4,0},{5,1},{6,2},{7,3},{8,4},{9,5},{1... | collective-permute-start | bytes 440 | tf_op jit(solution)/shard_map/ppermute | solution.py:19
  56.0 1.1 collective-permute-start.1
  57.2 2.3 %collective-permute-start = (bf16[1,9,8]{0,2,1:T(8,128)(2,1)S(1)}, bf16[1,9,8]{0,2,1:T(8,128)(2,1)S(1)}, u32[]{:S(2)}, u32[]{:S(2)}) collective-permute-start(bf16[1,9,8]{0,2,1:T(8,128)(2,1)S(1)} %get-tuple-element.96), channel_id=1, source_target_pairs={{0,15},{1,0},{2,1},{3,2},{4,3},{5,4},{6,5},{7,6},{8,7},{9,8},{10,9... | collective-permute-start | bytes 440 | tf_op jit(solution)/shard_map/ppermute | solution.py:19
  59.5 0.4 collective-permute-done.1
  59.9 1.1 collective-permute-done
  61.0 0.2 concatenate.6
  61.5 78.9 %while.10 = (s32[]{:T(128)}, f32[9,16,8]{1,0,2:T(8,128)S(1)}, s32[9,16,8]{1,0,2:T(8,128)S(1)}, s32[32]{0:T(128)S(1)}, bf16[9,16,32,128]{3,2,1,0:T(8,128)(2,1)}, ...) while((s32[]{:T(128)}, f32[9,16,8]{1,0,2:T(8,128)S(1)}, ...), condition=%wide.region_9.11_spmd, body=%wide.region_6.10_spmd.sunk | while | flops 135283968 | bytes 12794485 | solution.py:56
  61.7 1.2 gather_fusion.1
  63.1 3.0 %gather_fusion = bf16[128,128,128]{2,1,0:T(8,128)(2,1)} fusion(bf16[32,128,128]{2,1,0:T(8,128)(2,1)S(1)} %get-tuple-element.165, s32[1024]{0:T(1024)S(1)} %pad_clamp_fusion.4), kind=kCustom, calls=%fused_computation.1.clone.1 | custom fusion | bytes 8389120 | tf_op jit(solution)/shard_map/while/body/eval_jaxpr/gather | solution.py:54
  66.1 3.9 %select_reduce_fusion.3 = f32[16,32,8]{1,2,0:T(8,128)S(1)} fusion(bf16[16,8,128,128]{3,2,1,0:T(8,128)(2,1)} %bitcast.55, pred[16,8,128]{2,1,0:T(8,128)(4,1)S(1)} %iota_compare_fusion.7, bf16[9,16,32,128]{3,2,1,0:T(8,128)(2,1)} %get-tuple-element.164, s32[]{:T(128)S(6)} %copy.148), kind=kOutput, calls=%fused_computation.5.clone.1 | convolution fusion | flops 135262208 | bytes 4358148 | tf_op jit(solution)/shard_map/while/body/eval_jaxpr/mqd,mkpd->mqkp/dot_general | solution.py:34
  70.5 1.2 gather_fusion.1
  71.9 3.0 %gather_fusion = bf16[128,128,128]{2,1,0:T(8,128)(2,1)} fusion(bf16[32,128,128]{2,1,0:T(8,128)(2,1)S(1)} %get-tuple-element.165, s32[1024]{0:T(1024)S(1)} %pad_clamp_fusion.4), kind=kCustom, calls=%fused_computation.1.clone.1 | custom fusion | bytes 8389120 | tf_op jit(solution)/shard_map/while/body/eval_jaxpr/gather | solution.py:54
  74.9 3.9 %select_reduce_fusion.3 = f32[16,32,8]{1,2,0:T(8,128)S(1)} fusion(bf16[16,8,128,128]{3,2,1,0:T(8,128)(2,1)} %bitcast.55, pred[16,8,128]{2,1,0:T(8,128)(4,1)S(1)} %iota_compare_fusion.7, bf16[9,16,32,128]{3,2,1,0:T(8,128)(2,1)} %get-tuple-element.164, s32[]{:T(128)S(6)} %copy.148), kind=kOutput, calls=%fused_computation.5.clone.1 | convolution fusion | flops 135262208 | bytes 4358148 | tf_op jit(solution)/shard_map/while/body/eval_jaxpr/mqd,mkpd->mqkp/dot_general | solution.py:34
  79.2 1.2 gather_fusion.1
  80.7 3.0 %gather_fusion = bf16[128,128,128]{2,1,0:T(8,128)(2,1)} fusion(bf16[32,128,128]{2,1,0:T(8,128)(2,1)S(1)} %get-tuple-element.165, s32[1024]{0:T(1024)S(1)} %pad_clamp_fusion.4), kind=kCustom, calls=%fused_computation.1.clone.1 | custom fusion | bytes 8389120 | tf_op jit(solution)/shard_map/while/body/eval_jaxpr/gather | solution.py:54
  83.7 3.9 %select_reduce_fusion.3 = f32[16,32,8]{1,2,0:T(8,128)S(1)} fusion(bf16[16,8,128,128]{3,2,1,0:T(8,128)(2,1)} %bitcast.55, pred[16,8,128]{2,1,0:T(8,128)(4,1)S(1)} %iota_compare_fusion.7, bf16[9,16,32,128]{3,2,1,0:T(8,128)(2,1)} %get-tuple-element.164, s32[]{:T(128)S(6)} %copy.148), kind=kOutput, calls=%fused_computation.5.clone.1 | convolution fusion | flops 135262208 | bytes 4358148 | tf_op jit(solution)/shard_map/while/body/eval_jaxpr/mqd,mkpd->mqkp/dot_general | solution.py:34
  88.0 1.2 gather_fusion.1
  89.4 3.0 %gather_fusion = bf16[128,128,128]{2,1,0:T(8,128)(2,1)} fusion(bf16[32,128,128]{2,1,0:T(8,128)(2,1)S(1)} %get-tuple-element.165, s32[1024]{0:T(1024)S(1)} %pad_clamp_fusion.4), kind=kCustom, calls=%fused_computation.1.clone.1 | custom fusion | bytes 8389120 | tf_op jit(solution)/shard_map/while/body/eval_jaxpr/gather | solution.py:54
  92.4 3.9 %select_reduce_fusion.3 = f32[16,32,8]{1,2,0:T(8,128)S(1)} fusion(bf16[16,8,128,128]{3,2,1,0:T(8,128)(2,1)} %bitcast.55, pred[16,8,128]{2,1,0:T(8,128)(4,1)S(1)} %iota_compare_fusion.7, bf16[9,16,32,128]{3,2,1,0:T(8,128)(2,1)} %get-tuple-element.164, s32[]{:T(128)S(6)} %copy.148), kind=kOutput, calls=%fused_computation.5.clone.1 | convolution fusion | flops 135262208 | bytes 4358148 | tf_op jit(solution)/shard_map/while/body/eval_jaxpr/mqd,mkpd->mqkp/dot_general | solution.py:34
  96.8 1.2 gather_fusion.1
  98.2 3.0 %gather_fusion = bf16[128,128,128]{2,1,0:T(8,128)(2,1)} fusion(bf16[32,128,128]{2,1,0:T(8,128)(2,1)S(1)} %get-tuple-element.165, s32[1024]{0:T(1024)S(1)} %pad_clamp_fusion.4), kind=kCustom, calls=%fused_computation.1.clone.1 | custom fusion | bytes 8389120 | tf_op jit(solution)/shard_map/while/body/eval_jaxpr/gather | solution.py:54
  101.2 3.9 %select_reduce_fusion.3 = f32[16,32,8]{1,2,0:T(8,128)S(1)} fusion(bf16[16,8,128,128]{3,2,1,0:T(8,128)(2,1)} %bitcast.55, pred[16,8,128]{2,1,0:T(8,128)(4,1)S(1)} %iota_compare_fusion.7, bf16[9,16,32,128]{3,2,1,0:T(8,128)(2,1)} %get-tuple-element.164, s32[]{:T(128)S(6)} %copy.148), kind=kOutput, calls=%fused_computation.5.clone.1 | convolution fusion | flops 135262208 | bytes 4358148 | tf_op jit(solution)/shard_map/while/body/eval_jaxpr/mqd,mkpd->mqkp/dot_general | solution.py:34
  105.5 1.2 gather_fusion.1
  106.9 3.0 %gather_fusion = bf16[128,128,128]{2,1,0:T(8,128)(2,1)} fusion(bf16[32,128,128]{2,1,0:T(8,128)(2,1)S(1)} %get-tuple-element.165, s32[1024]{0:T(1024)S(1)} %pad_clamp_fusion.4), kind=kCustom, calls=%fused_computation.1.clone.1 | custom fusion | bytes 8389120 | tf_op jit(solution)/shard_map/while/body/eval_jaxpr/gather | solution.py:54
  110.0 3.9 %select_reduce_fusion.3 = f32[16,32,8]{1,2,0:T(8,128)S(1)} fusion(bf16[16,8,128,128]{3,2,1,0:T(8,128)(2,1)} %bitcast.55, pred[16,8,128]{2,1,0:T(8,128)(4,1)S(1)} %iota_compare_fusion.7, bf16[9,16,32,128]{3,2,1,0:T(8,128)(2,1)} %get-tuple-element.164, s32[]{:T(128)S(6)} %copy.148), kind=kOutput, calls=%fused_computation.5.clone.1 | convolution fusion | flops 135262208 | bytes 4358148 | tf_op jit(solution)/shard_map/while/body/eval_jaxpr/mqd,mkpd->mqkp/dot_general | solution.py:34
  114.3 1.2 gather_fusion.1
  115.7 3.0 %gather_fusion = bf16[128,128,128]{2,1,0:T(8,128)(2,1)} fusion(bf16[32,128,128]{2,1,0:T(8,128)(2,1)S(1)} %get-tuple-element.165, s32[1024]{0:T(1024)S(1)} %pad_clamp_fusion.4), kind=kCustom, calls=%fused_computation.1.clone.1 | custom fusion | bytes 8389120 | tf_op jit(solution)/shard_map/while/body/eval_jaxpr/gather | solution.py:54
  118.7 3.9 %select_reduce_fusion.3 = f32[16,32,8]{1,2,0:T(8,128)S(1)} fusion(bf16[16,8,128,128]{3,2,1,0:T(8,128)(2,1)} %bitcast.55, pred[16,8,128]{2,1,0:T(8,128)(4,1)S(1)} %iota_compare_fusion.7, bf16[9,16,32,128]{3,2,1,0:T(8,128)(2,1)} %get-tuple-element.164, s32[]{:T(128)S(6)} %copy.148), kind=kOutput, calls=%fused_computation.5.clone.1 | convolution fusion | flops 135262208 | bytes 4358148 | tf_op jit(solution)/shard_map/while/body/eval_jaxpr/mqd,mkpd->mqkp/dot_general | solution.py:34
  123.1 1.2 gather_fusion.1
  124.5 3.0 %gather_fusion = bf16[128,128,128]{2,1,0:T(8,128)(2,1)} fusion(bf16[32,128,128]{2,1,0:T(8,128)(2,1)S(1)} %get-tuple-element.165, s32[1024]{0:T(1024)S(1)} %pad_clamp_fusion.4), kind=kCustom, calls=%fused_computation.1.clone.1 | custom fusion | bytes 8389120 | tf_op jit(solution)/shard_map/while/body/eval_jaxpr/gather | solution.py:54
  127.5 3.9 %select_reduce_fusion.3 = f32[16,32,8]{1,2,0:T(8,128)S(1)} fusion(bf16[16,8,128,128]{3,2,1,0:T(8,128)(2,1)} %bitcast.55, pred[16,8,128]{2,1,0:T(8,128)(4,1)S(1)} %iota_compare_fusion.7, bf16[9,16,32,128]{3,2,1,0:T(8,128)(2,1)} %get-tuple-element.164, s32[]{:T(128)S(6)} %copy.148), kind=kOutput, calls=%fused_computation.5.clone.1 | convolution fusion | flops 135262208 | bytes 4358148 | tf_op jit(solution)/shard_map/while/body/eval_jaxpr/mqd,mkpd->mqkp/dot_general | solution.py:34
  131.8 1.2 gather_fusion.1
  133.2 3.0 %gather_fusion = bf16[128,128,128]{2,1,0:T(8,128)(2,1)} fusion(bf16[32,128,128]{2,1,0:T(8,128)(2,1)S(1)} %get-tuple-element.165, s32[1024]{0:T(1024)S(1)} %pad_clamp_fusion.4), kind=kCustom, calls=%fused_computation.1.clone.1 | custom fusion | bytes 8389120 | tf_op jit(solution)/shard_map/while/body/eval_jaxpr/gather | solution.py:54
  136.3 3.9 %select_reduce_fusion.3 = f32[16,32,8]{1,2,0:T(8,128)S(1)} fusion(bf16[16,8,128,128]{3,2,1,0:T(8,128)(2,1)} %bitcast.55, pred[16,8,128]{2,1,0:T(8,128)(4,1)S(1)} %iota_compare_fusion.7, bf16[9,16,32,128]{3,2,1,0:T(8,128)(2,1)} %get-tuple-element.164, s32[]{:T(128)S(6)} %copy.148), kind=kOutput, calls=%fused_computation.5.clone.1 | convolution fusion | flops 135262208 | bytes 4358148 | tf_op jit(solution)/shard_map/while/body/eval_jaxpr/mqd,mkpd->mqkp/dot_general | solution.py:34
  140.5 0.7 copy.120
  141.1 5.8 %all-to-all-start.1 = ((f32[16,9,8]{1,2,0:T(8,128)}), f32[16,9,8]{1,2,0:T(8,128)S(1)}, u32[]{:S(2)}, u32[]{:S(2)}) async-start(f32[16,9,8]{1,2,0:T(8,128)} %copy.120), calls=%async_computation.1 | async-start | bytes 131072 | tf_op jit(solution)/shard_map/all_to_all | solution.py:140
  147.0 6.9 %all-to-all-done.1 = f32[16,9,8]{1,2,0:T(8,128)S(1)} async-done(((f32[16,9,8]{1,2,0:T(8,128)}), f32[16,9,8]{1,2,0:T(8,128)S(1)}, u32[]{:S(2)}, u32[]{:S(2)}) %all-to-all-start.1) | async-done | bytes 4640 | tf_op jit(solution)/shard_map/all_to_all | solution.py:140
  153.8 0.2 copy.121
  154.1 4.5 %gather_fusion.3 = f32[768]{0:T(1024)S(1)} fusion(f32[1152]{0:T(1024)S(1)} %reshape.259, s32[1024]{0:T(1024)S(1)} %pad_clamp_fusion.1), kind=kCustom, calls=%fused_computation.3 | custom fusion | bytes 9216 | tf_op jit(solution)/shard_map/jit(_take)/gather | solution.py:144
  158.8 0.7 copy.129
  (159 shorter events, 7.4 us)
Async XLA Ops:
  0.0 1.7 %copy-start = (s32[512]{0:T(512)S(1)}, s32[512]{0:T(512)}, u32[]{:S(2)}) copy-start(s32[512]{0:T(512)} %param.15) | copy-start | bytes 6148
  1.7 5.5 %copy-start.3 = (bf16[32,32,128]{2,1,0:T(8,128)(2,1)S(1)}, bf16[32,32,128]{2,1,0:T(8,128)(2,1)}, u32[]{:S(2)}) copy-start(bf16[32,32,128]{2,1,0:T(8,128)(2,1)} %param.12) | copy-start | bytes 786436
  9.0 52.4 %all-to-all-start = ((bf16[16,9,32,128]{3,2,1,0:T(8,128)(2,1)}), bf16[16,9,32,128]{3,2,1,0:T(8,128)(2,1)}, u32[]{:S(2)}, u32[]{:S(2)}) async-start(bf16[16,9,32,128]{3,2,1,0:T(8,128)(2,1)} %copy.117), calls=%async_computation | async-start | bytes 2359296 | tf_op jit(solution)/shard_map/all_to_all | solution.py:131
  20.7 21.7 %collective-permute-start.14 = (bf16[1,9,8]{0,2,1:T(8,128)(2,1)}, bf16[1,9,8]{0,2,1:T(8,128)(2,1)S(1)}, u32[]{:S(2)}, u32[]{:S(2)}) collective-permute-start(bf16[1,9,8]{0,2,1:T(8,128)(2,1)} %get-tuple-element.82), channel_id=1, source_target_pairs={{0,1},{1,2},{2,3},{3,4},{4,5},{5,6},{6,7},{7,8},{8,9},{9,10},{10,1... | collective-permute-start | bytes 440 | tf_op jit(solution)/shard_map/ppermute | solution.py:19
  21.0 22.9 %collective-permute-start.13 = (bf16[1,9,8]{0,2,1:T(8,128)(2,1)}, bf16[1,9,8]{0,2,1:T(8,128)(2,1)S(1)}, u32[]{:S(2)}, u32[]{:S(2)}) collective-permute-start(bf16[1,9,8]{0,2,1:T(8,128)(2,1)} %get-tuple-element.83), channel_id=1, source_target_pairs={{0,2},{1,3},{2,4},{3,5},{4,6},{5,7},{6,8},{7,9},{8,10},{9,11},{10,... | collective-permute-start | bytes 440 | tf_op jit(solution)/shard_map/ppermute | solution.py:19
  22.6 25.3 %collective-permute-start.12 = (bf16[1,9,8]{0,2,1:T(8,128)(2,1)}, bf16[1,9,8]{0,2,1:T(8,128)(2,1)S(1)}, u32[]{:S(2)}, u32[]{:S(2)}) collective-permute-start(bf16[1,9,8]{0,2,1:T(8,128)(2,1)} %get-tuple-element.84), channel_id=1, source_target_pairs={{0,3},{1,4},{2,5},{3,6},{4,7},{5,8},{6,9},{7,10},{8,11},{9,12},{10... | collective-permute-start | bytes 440 | tf_op jit(solution)/shard_map/ppermute | solution.py:19
  24.9 23.7 %collective-permute-start.11 = (bf16[1,9,8]{0,2,1:T(8,128)(2,1)}, bf16[1,9,8]{0,2,1:T(8,128)(2,1)S(1)}, u32[]{:S(2)}, u32[]{:S(2)}) collective-permute-start(bf16[1,9,8]{0,2,1:T(8,128)(2,1)} %get-tuple-element.85), channel_id=1, source_target_pairs={{0,4},{1,5},{2,6},{3,7},{4,8},{5,9},{6,10},{7,11},{8,12},{9,13},{1... | collective-permute-start | bytes 440 | tf_op jit(solution)/shard_map/ppermute | solution.py:19
  26.4 24.4 %collective-permute-start.10 = (bf16[1,9,8]{0,2,1:T(8,128)(2,1)}, bf16[1,9,8]{0,2,1:T(8,128)(2,1)S(1)}, u32[]{:S(2)}, u32[]{:S(2)}) collective-permute-start(bf16[1,9,8]{0,2,1:T(8,128)(2,1)} %get-tuple-element.86), channel_id=1, source_target_pairs={{0,5},{1,6},{2,7},{3,8},{4,9},{5,10},{6,11},{7,12},{8,13},{9,14},{... | collective-permute-start | bytes 440 | tf_op jit(solution)/shard_map/ppermute | solution.py:19
  26.9 5.4 %copy-start.4 = (f32[4]{0:T(128)S(1)}, f32[4]{0:T(128)}, u32[]{:S(2)}) copy-start(f32[4]{0:T(128)} %param.19) | copy-start | bytes 52
  26.9 6.1 %copy-start.2 = (s32[32,128,128]{2,1,0:T(8,128)S(1)}, s32[32,128,128]{2,1,0:T(8,128)}, u32[]{:S(2)}) copy-start(s32[32,128,128]{2,1,0:T(8,128)} %param.17) | copy-start | bytes 6291460
  37.7 23.7 %copy-start.1 = (s32[32]{0:T(128)S(1)}, s32[32]{0:T(128)}, u32[]{:S(2)}) copy-start(s32[32]{0:T(128)} %param.18) | copy-start | bytes 388
  42.4 11.0 %collective-permute-start.9 = (bf16[1,9,8]{0,2,1:T(8,128)(2,1)}, bf16[1,9,8]{0,2,1:T(8,128)(2,1)S(1)}, u32[]{:S(2)}, u32[]{:S(2)}) collective-permute-start(bf16[1,9,8]{0,2,1:T(8,128)(2,1)} %get-tuple-element.87), channel_id=1, source_target_pairs={{0,6},{1,7},{2,8},{3,9},{4,10},{5,11},{6,12},{7,13},{8,14},{9,15},... | collective-permute-start | bytes 440 | tf_op jit(solution)/shard_map/ppermute | solution.py:19
  43.9 10.3 %collective-permute-start.8 = (bf16[1,9,8]{0,2,1:T(8,128)(2,1)S(1)}, bf16[1,9,8]{0,2,1:T(8,128)(2,1)S(1)}, u32[]{:S(2)}, u32[]{:S(2)}) collective-permute-start(bf16[1,9,8]{0,2,1:T(8,128)(2,1)S(1)} %get-tuple-element.88), channel_id=1, source_target_pairs={{0,7},{1,8},{2,9},{3,10},{4,11},{5,12},{6,13},{7,14},{8,15},{9,0},... | collective-permute-start | bytes 440 | tf_op jit(solution)/shard_map/ppermute | solution.py:19
  48.0 8.0 %collective-permute-start.7 = (bf16[1,9,8]{0,2,1:T(8,128)(2,1)S(1)}, bf16[1,9,8]{0,2,1:T(8,128)(2,1)S(1)}, u32[]{:S(2)}, u32[]{:S(2)}) collective-permute-start(bf16[1,9,8]{0,2,1:T(8,128)(2,1)S(1)} %get-tuple-element.89), channel_id=1, source_target_pairs={{0,8},{1,9},{2,10},{3,11},{4,12},{5,13},{6,14},{7,15},{8,0},{9,1},... | collective-permute-start | bytes 440 | tf_op jit(solution)/shard_map/ppermute | solution.py:19
  48.5 7.5 %collective-permute-start.6 = (bf16[1,9,8]{0,2,1:T(8,128)(2,1)S(1)}, bf16[1,9,8]{0,2,1:T(8,128)(2,1)S(1)}, u32[]{:S(2)}, u32[]{:S(2)}) collective-permute-start(bf16[1,9,8]{0,2,1:T(8,128)(2,1)S(1)} %get-tuple-element.90), channel_id=1, source_target_pairs={{0,9},{1,10},{2,11},{3,12},{4,13},{5,14},{6,15},{7,0},{8,1},{9,2},... | collective-permute-start | bytes 440 | tf_op jit(solution)/shard_map/ppermute | solution.py:19
  50.8 6.4 %collective-permute-start.5 = (bf16[1,9,8]{0,2,1:T(8,128)(2,1)S(1)}, bf16[1,9,8]{0,2,1:T(8,128)(2,1)S(1)}, u32[]{:S(2)}, u32[]{:S(2)}) collective-permute-start(bf16[1,9,8]{0,2,1:T(8,128)(2,1)S(1)} %get-tuple-element.91), channel_id=1, source_target_pairs={{0,10},{1,11},{2,12},{3,13},{4,14},{5,15},{6,0},{7,1},{8,2},{9,3},... | collective-permute-start | bytes 440 | tf_op jit(solution)/shard_map/ppermute | solution.py:19
  53.4 6.1 %collective-permute-start.4 = (bf16[1,9,8]{0,2,1:T(8,128)(2,1)S(1)}, bf16[1,9,8]{0,2,1:T(8,128)(2,1)S(1)}, u32[]{:S(2)}, u32[]{:S(2)}) collective-permute-start(bf16[1,9,8]{0,2,1:T(8,128)(2,1)S(1)} %get-tuple-element.92), channel_id=1, source_target_pairs={{0,11},{1,12},{2,13},{3,14},{4,15},{5,0},{6,1},{7,2},{8,3},{9,4},{... | collective-permute-start | bytes 440 | tf_op jit(solution)/shard_map/ppermute | solution.py:19
  54.2 5.3 %collective-permute-start.3 = (bf16[1,9,8]{0,2,1:T(8,128)(2,1)S(1)}, bf16[1,9,8]{0,2,1:T(8,128)(2,1)S(1)}, u32[]{:S(2)}, u32[]{:S(2)}) collective-permute-start(bf16[1,9,8]{0,2,1:T(8,128)(2,1)S(1)} %get-tuple-element.93), channel_id=1, source_target_pairs={{0,12},{1,13},{2,14},{3,15},{4,0},{5,1},{6,2},{7,3},{8,4},{9,5},{1... | collective-permute-start | bytes 440 | tf_op jit(solution)/shard_map/ppermute | solution.py:19
  56.0 3.5 %collective-permute-start.2 = (bf16[1,9,8]{0,2,1:T(8,128)(2,1)S(1)}, bf16[1,9,8]{0,2,1:T(8,128)(2,1)S(1)}, u32[]{:S(2)}, u32[]{:S(2)}) collective-permute-start(bf16[1,9,8]{0,2,1:T(8,128)(2,1)S(1)} %get-tuple-element.94), channel_id=1, source_target_pairs={{0,13},{1,14},{2,15},{3,0},{4,1},{5,2},{6,3},{7,4},{8,5},{9,6},{10... | collective-permute-start | bytes 440 | tf_op jit(solution)/shard_map/ppermute | solution.py:19
  56.0 3.8 %collective-permute-start.1 = (bf16[1,9,8]{0,2,1:T(8,128)(2,1)S(1)}, bf16[1,9,8]{0,2,1:T(8,128)(2,1)S(1)}, u32[]{:S(2)}, u32[]{:S(2)}) collective-permute-start(bf16[1,9,8]{0,2,1:T(8,128)(2,1)S(1)} %get-tuple-element.95), channel_id=1, source_target_pairs={{0,14},{1,15},{2,0},{3,1},{4,2},{5,3},{6,4},{7,5},{8,6},{9,7},{10,... | collective-permute-start | bytes 440 | tf_op jit(solution)/shard_map/ppermute | solution.py:19
  57.2 3.8 %collective-permute-start = (bf16[1,9,8]{0,2,1:T(8,128)(2,1)S(1)}, bf16[1,9,8]{0,2,1:T(8,128)(2,1)S(1)}, u32[]{:S(2)}, u32[]{:S(2)}) collective-permute-start(bf16[1,9,8]{0,2,1:T(8,128)(2,1)S(1)} %get-tuple-element.96), channel_id=1, source_target_pairs={{0,15},{1,0},{2,1},{3,2},{4,3},{5,4},{6,5},{7,6},{8,7},{9,8},{10,9... | collective-permute-start | bytes 440 | tf_op jit(solution)/shard_map/ppermute | solution.py:19
  141.1 12.7 %all-to-all-start.1 = ((f32[16,9,8]{1,2,0:T(8,128)}), f32[16,9,8]{1,2,0:T(8,128)S(1)}, u32[]{:S(2)}, u32[]{:S(2)}) async-start(f32[16,9,8]{1,2,0:T(8,128)} %copy.120), calls=%async_computation.1 | async-start | bytes 131072 | tf_op jit(solution)/shard_map/all_to_all | solution.py:140
  154.1 4.6 %copy-start.5 = (s32[32]{0:T(128)S(1)}, s32[32]{0:T(128)}, u32[]{:S(2)}) copy-start(s32[32]{0:T(128)} %param.14) | copy-start | bytes 388
